TPU v7x, 256 devices: a whole 4x4x8 slice. The times are simulated.
256 devices in a mesh: col: 32 (over x, y, core), sub: 8 (over z).
Axes of the slice: x: 4, y: 4, z: 8, core: 2. Of those that a mesh axis runs over, the one named last changes fastest.
Arguments:
- vectors: bfloat16 [1048576, 128], P(('col', 'sub')), may hold values from -6 to 6
- near_blocks: bfloat16 [4096, 4, 256, 256], P(('col', 'sub')), may hold values from -0.1875 to 0.1875
- near_index: int32 [4096, 4], P(('col', 'sub')), may hold values from 0 to 4095, as said below
- leaf_basis: bfloat16 [4096, 32, 256], P(('col', 'sub')), may hold values from -0.375 to 0.375
- leaf_transfer: float32 [4096, 32, 32], P(('col', 'sub')), may hold values from -0.25 to 0.25
- leaf_coupling: float32 [4096, 8, 32, 32], P(('col', 'sub')), may hold values from -0.375 to 0.375
- leaf_far: int32 [4096, 8], P(('col', 'sub')), may hold values from 0 to 4095, as said below
- cluster_transfer: float32 [256, 32, 32], P(('col', 'sub')), may hold values from -0.375 to 0.375
- cluster_coupling: float32 [256, 4, 32, 32], P(('col', 'sub')), may hold values from -0.5 to 0.5
- cluster_partner: int32 [256, 4], P(('col', 'sub')), may hold values from 0 to 7
- top_coupling: float32 [32, 8, 32, 32], P('col'), may hold values from -0.375 to 0.375
- top_partner: int32 [32, 8], P('col'), may hold values from 0 to 31
Outputs:
- products: bfloat16 [1048576, 128], P(('col', 'sub'))
Inputs may be any that keep to these rules, and one draw needn't show every extreme that they name: `near_index`: slot 0 of leaf i is i itself; every entry lies within 16 leaves of i; slot 1 is exactly 16 leaves away from i. `leaf_far`: every entry lies within 16 leaves of its row leaf i; slots 0 and 1 are exactly 16 leaves away from i.
All inputs are finite; a program needn't handle non-finite values.
Results may differ from a plain program's by a relative error of at most 0.0034.
Values may be sent and summed in bfloat16 or wider, within the bound.
A program may use at most 64 MiB of HBM per device.

v0:
```python
import jax
import jax.numpy as jnp
from jax import lax
from jax.sharding import PartitionSpec as P

HIGHEST = lax.Precision.HIGHEST


def with_halo(block, sides, width):
    for axis, dim in sides:
        count = lax.axis_size(axis)
        forward = [(i, i + 1) for i in range(count - 1)]
        backward = [(target, source) for source, target in forward]
        low = lax.ppermute(
            lax.slice_in_dim(block, block.shape[dim] - width, None, axis=dim), axis, forward
        )
        high = lax.ppermute(lax.slice_in_dim(block, 0, width, axis=dim), axis, backward)
        block = jnp.concatenate([low, block, high], axis=dim)
    return block


def local(
    vectors,
    near_blocks,
    near_index,
    leaf_basis,
    leaf_transfer,
    leaf_coupling,
    leaf_far,
    cluster_transfer,
    cluster_coupling,
    cluster_partner,
    top_coupling,
    top_partner,
):
    leaves_here = leaf_basis.shape[0]
    leaf_rows = leaf_basis.shape[2]
    columns = vectors.shape[1]
    window_start = lax.axis_index(("col", "sub")) * leaves_here - leaves_here
    widened = with_halo(vectors, ((("col", "sub"), 0),), leaves_here * leaf_rows)
    window_vec = widened.reshape(3 * leaves_here, leaf_rows, columns)
    own_vec = vectors.reshape(leaves_here, leaf_rows, columns)
    leaf_coefs = jnp.einsum("lrp,lpc->lrc", leaf_basis, own_vec, preferred_element_type=jnp.float32)
    window_coefs = with_halo(leaf_coefs, ((("col", "sub"), 0),), leaves_here)
    cluster_coef = jnp.einsum("lrs,lrc->sc", leaf_transfer, leaf_coefs, precision=HIGHEST)
    sub_coefs = lax.all_gather(cluster_coef[None], "sub", axis=0, tiled=True)
    cluster_field = jnp.einsum(
        "krs,ksc->rc", cluster_coupling[0], sub_coefs[cluster_partner[0]], precision=HIGHEST
    )
    upward = jnp.dot(cluster_transfer[0].T, cluster_coef, precision=HIGHEST)
    top_coef = lax.psum(upward, "sub")
    col_coefs = lax.all_gather(top_coef[None], "col", axis=0, tiled=True)
    top_field = jnp.einsum(
        "krs,ksc->rc", top_coupling[0], col_coefs[top_partner[0]], precision=HIGHEST
    )
    cluster_field = cluster_field + jnp.dot(cluster_transfer[0], top_field, precision=HIGHEST)
    far_coefs = window_coefs[leaf_far - window_start]
    leaf_field = jnp.einsum("lkrs,lksc->lrc", leaf_coupling, far_coefs, precision=HIGHEST)
    leaf_field = leaf_field + jnp.einsum(
        "lrs,sc->lrc", leaf_transfer, cluster_field, precision=HIGHEST
    )
    rounded = leaf_field.astype(jnp.bfloat16)
    picked = window_vec[near_index - window_start]
    near_part = jnp.einsum(
        "lkij,lkjc->lic", near_blocks, picked, preferred_element_type=jnp.float32
    )
    far_part = jnp.einsum("lrp,lrc->lpc", leaf_basis, rounded, preferred_element_type=jnp.float32)
    return (near_part + far_part).astype(jnp.bfloat16).reshape(leaves_here * leaf_rows, columns)


def solution(mesh):
    in_specs = (
        P(("col", "sub"), None),
        P(("col", "sub"), None, None, None),
        P(("col", "sub"), None),
        P(("col", "sub"), None, None),
        P(("col", "sub"), None, None),
        P(("col", "sub"), None, None, None),
        P(("col", "sub"), None),
        P(("col", "sub"), None, None),
        P(("col", "sub"), None, None, None),
        P(("col", "sub"), None),
        P("col", None, None, None),
        P("col", None),
    )
    out_specs = P(("col", "sub"), None)
    return jax.shard_map(local, mesh=mesh, in_specs=in_specs, out_specs=out_specs, check_vma=False)
```

profile of v0, /device:TPU:1, one launch (start us, length us, event | category | flops | bytes accessed | tf_op | source)
XLA Modules:
  0.0 154.2 jit_solution(7868082268854348627)
XLA Ops:
  0.0 1.7 %fusion.12 = f32[16,32,128]{2,1,0:T(8,128)S(1)} fusion(bf16[16,32,256]{2,1,0:T(8,128)(2,1)} %param.15, bf16[16,256,128]{2,1,0:T(8,128)(2,1)} %bitcast.79), kind=kOutput, calls=%fused_computation.33 | convolution fusion | flops 33554432 | bytes 1572864 | tf_op jit(solution)/shard_map/lrp,lpc->lrc/dot_general | solution.py:43
  1.7 8.9 %collective-permute-start.3 = (f32[16,32,128]{2,1,0:T(8,128)S(1)}, f32[16,32,128]{2,1,0:T(8,128)S(1)}, u32[]{:S(2)}, u32[]{:S(2)}) collective-permute-start(f32[16,32,128]{2,1,0:T(8,128)S(1)} %fusion.12), channel_id=1, source_target_pairs={{1,0},{2,1},{3,2},{4,3},{5,4},{6,5},{7,6},{8,7},{9,8},{10,9},{11,1... | collective-permute-start | bytes 786440 | tf_op jit(solution)/shard_map/ppermute | solution.py:17
  10.6 1.9 %collective-permute-start.2 = (f32[16,32,128]{2,1,0:T(8,128)S(1)}, f32[16,32,128]{2,1,0:T(8,128)}, u32[]{:S(2)}, u32[]{:S(2)}) collective-permute-start(f32[16,32,128]{2,1,0:T(8,128)S(1)} %fusion.12), channel_id=1, source_target_pairs={{0,1},{1,2},{2,3},{3,4},{4,5},{5,6},{6,7},{7,8},{8,9},{9,10},{10,1... | collective-permute-start | bytes 786440 | tf_op jit(solution)/shard_map/ppermute | solution.py:14
  12.5 4.9 %collective-permute-start.1 = (bf16[4096,128]{1,0:T(8,128)(2,1)}, bf16[4096,128]{1,0:T(8,128)(2,1)}, u32[]{:S(2)}, u32[]{:S(2)}) collective-permute-start(bf16[4096,128]{1,0:T(8,128)(2,1)} %param.12), channel_id=1, source_target_pairs={{1,0},{2,1},{3,2},{4,3},{5,4},{6,5},{7,6},{8,7},{9,8},{10,9},{11,1... | collective-permute-start | bytes 3145736 | tf_op jit(solution)/shard_map/ppermute | solution.py:17
  17.4 1.9 %collective-permute-start = (bf16[4096,128]{1,0:T(8,128)(2,1)}, bf16[4096,128]{1,0:T(8,128)(2,1)}, u32[]{:S(2)}, u32[]{:S(2)}) collective-permute-start(bf16[4096,128]{1,0:T(8,128)(2,1)} %param.12), channel_id=1, source_target_pairs={{0,1},{1,2},{2,3},{3,4},{4,5},{5,6},{6,7},{7,8},{8,9},{9,10},{10,1... | collective-permute-start | bytes 3145736 | tf_op jit(solution)/shard_map/ppermute | solution.py:14
  19.3 0.7 fusion.10
  20.7 1.3 compare_select_fusion.1
  21.9 0.7 compare_select_fusion
  23.9 1.5 fusion.13
  25.4 0.9 convolution_bitcast_fusion.3
  26.4 35.0 %psum.7 = f32[1,32,128]{2,1,0:T(8,128)S(1)} all-reduce(f32[1,32,128]{2,1,0:T(8,128)S(1)} %convolution_bitcast_fusion.3), channel_id=1, replica_groups=mesh['col'=32,'sub'=8] {'sub'}, use_global_device_ids=true, to_apply=%region_0.0 | all-reduce | flops 4096 | bytes 32768 | tf_op jit(solution)/shard_map/psum | solution.py:51
  61.4 18.5 %all-gather = f32[256,128]{1,0:T(8,128)S(1)} all-gather(f32[32,128]{1,0:T(8,128)S(1)} %bitcast.81), channel_id=2, replica_groups=mesh['col'=32,'sub'=8] {'sub'}, dimensions={0}, use_global_device_ids=true | all-gather | bytes 147456 | tf_op jit(solution)/shard_map/all_gather | solution.py:46
  79.9 36.2 %all_gather.7 = f32[32,32,128]{2,1,0:T(8,128)S(1)} all-gather(f32[1,32,128]{2,1,0:T(8,128)S(1)} %psum.7), channel_id=1, replica_groups=mesh['col'=32,'sub'=8] {'col'}, dimensions={0}, use_global_device_ids=true | all-gather | bytes 540672 | tf_op jit(solution)/shard_map/all_gather | solution.py:52
  116.9 0.7 gather_fusion.3
  118.5 0.7 copy.22
  119.4 0.9 fusion.4
  120.3 1.0 pad_maximum_fusion.1
  121.3 2.1 %gather_fusion.1 = f32[128,32,128]{2,1,0:T(8,128)} fusion(f32[48,32,128]{2,1,0:T(8,128)S(1)} %pad_maximum_fusion.1, s32[1024]{0:T(1024)S(1)} %pad_clamp_fusion.2), kind=kCustom, calls=%fused_computation.1 | custom fusion | bytes 4194816 | tf_op jit(solution)/shard_map/gather | solution.py:57
  123.4 4.4 %convolution_bitcast_fusion.1 = f32[16,32,128]{2,1,0:T(8,128)S(1)} fusion(f32[16,8,32,128]{3,2,1,0:T(8,128)} %bitcast.78, f32[16,8,32,32]{3,2,1,0:T(8,128)S(1)} %copy-done), kind=kOutput, calls=%fused_computation.10 | convolution fusion | flops 201326592 | bytes 2883584 | tf_op jit(solution)/shard_map/lkrs,lksc->lrc/dot_general | solution.py:58
  128.2 1.9 %fusion.14 = f32[16,128,256]{2,1,0:T(8,128)} fusion(bf16[16,32,128]{2,1,0:T(8,128)(2,1)S(1)} %fusion.3, bf16[16,32,256]{2,1,0:T(8,128)(2,1)S(1)} %copy-done.2), kind=kOutput, calls=%fused_computation.35 | convolution fusion | flops 33554432 | bytes 2490368 | tf_op jit(solution)/shard_map/lrp,lrc->lpc/dot_general | solution.py:67
  130.1 9.8 %pad_maximum_fusion = bf16[12288,128]{1,0:T(8,128)(2,1)} fusion(bf16[4096,128]{1,0:T(8,128)(2,1)} %collective-permute-done.1, bf16[4096,128]{1,0:T(8,128)(2,1)S(1)} %copy-done.1, bf16[4096,128]{1,0:T(8,128)(2,1)} %collective-permute-done), kind=kLoop, calls=%fused_computation.4 | loop fusion | flops 9437184 | bytes 6291456 | tf_op jit(solution)/shard_map/concatenate | solution.py:18
  139.9 4.9 %gather_fusion = bf16[64,256,128]{2,1,0:T(8,128)(2,1)} fusion(bf16[48,256,128]{2,1,0:T(8,128)(2,1)} %bitcast.76, s32[1024]{0:T(1024)S(1)} %pad_clamp_fusion.3), kind=kCustom, calls=%fused_computation | custom fusion | bytes 8388864 | tf_op jit(solution)/shard_map/gather | solution.py:63
  144.8 8.1 %fusion.1 = bf16[16,256,128]{1,2,0:T(8,128)(2,1)S(1)} fusion(f32[16,128,256]{2,1,0:T(8,128)} %fusion.14, bf16[16,4,256,128]{3,2,1,0:T(8,128)(2,1)} %bitcast.77, bf16[16,4,256,256]{3,2,1,0:T(8,128)(2,1)} %param.13), kind=kOutput, calls=%fused_computation.7 | convolution fusion | flops 1074790400 | bytes 15728640 | tf_op jit(solution)/shard_map/lkij,lkjc->lic/dot_general | solution.py:64
  152.9 1.3 copy.26
  (28 shorter events, 4.2 us)
Async XLA Ops:
  0.0 123.4 %copy-start = (f32[16,8,32,32]{3,2,1,0:T(8,128)S(1)}, f32[16,8,32,32]{3,2,1,0:T(8,128)}, u32[]{:S(2)}) copy-start(f32[16,8,32,32]{3,2,1,0:T(8,128)} %param.17) | copy-start | bytes 1572868
  0.0 116.6 %copy-start.5 = (f32[1,4,32,32]{3,2,1,0:T(8,128)S(1)}, f32[1,4,32,32]{3,2,1,0:T(8,128)}, u32[]{:S(2)}) copy-start(f32[1,4,32,32]{3,2,1,0:T(8,128)} %param.20) | copy-start | bytes 49156
  0.0 117.6 %copy-start.4 = (f32[1,8,32,32]{3,2,1,0:T(8,128)S(1)}, f32[1,8,32,32]{3,2,1,0:T(8,128)}, u32[]{:S(2)}) copy-start(f32[1,8,32,32]{3,2,1,0:T(8,128)} %param.22) | copy-start | bytes 98308
  1.7 118.5 %collective-permute-start.3 = (f32[16,32,128]{2,1,0:T(8,128)S(1)}, f32[16,32,128]{2,1,0:T(8,128)S(1)}, u32[]{:S(2)}, u32[]{:S(2)}) collective-permute-start(f32[16,32,128]{2,1,0:T(8,128)S(1)} %fusion.12), channel_id=1, source_target_pairs={{1,0},{2,1},{3,2},{4,3},{5,4},{6,5},{7,6},{8,7},{9,8},{10,9},{11,1... | collective-permute-start | bytes 786440 | tf_op jit(solution)/shard_map/ppermute | solution.py:17
  10.6 109.6 %collective-permute-start.2 = (f32[16,32,128]{2,1,0:T(8,128)S(1)}, f32[16,32,128]{2,1,0:T(8,128)}, u32[]{:S(2)}, u32[]{:S(2)}) collective-permute-start(f32[16,32,128]{2,1,0:T(8,128)S(1)} %fusion.12), channel_id=1, source_target_pairs={{0,1},{1,2},{2,3},{3,4},{4,5},{5,6},{6,7},{7,8},{8,9},{9,10},{10,1... | collective-permute-start | bytes 786440 | tf_op jit(solution)/shard_map/ppermute | solution.py:14
  12.5 117.6 %collective-permute-start.1 = (bf16[4096,128]{1,0:T(8,128)(2,1)}, bf16[4096,128]{1,0:T(8,128)(2,1)}, u32[]{:S(2)}, u32[]{:S(2)}) collective-permute-start(bf16[4096,128]{1,0:T(8,128)(2,1)} %param.12), channel_id=1, source_target_pairs={{1,0},{2,1},{3,2},{4,3},{5,4},{6,5},{7,6},{8,7},{9,8},{10,9},{11,1... | collective-permute-start | bytes 3145736 | tf_op jit(solution)/shard_map/ppermute | solution.py:17
  17.4 112.7 %collective-permute-start = (bf16[4096,128]{1,0:T(8,128)(2,1)}, bf16[4096,128]{1,0:T(8,128)(2,1)}, u32[]{:S(2)}, u32[]{:S(2)}) collective-permute-start(bf16[4096,128]{1,0:T(8,128)(2,1)} %param.12), channel_id=1, source_target_pairs={{0,1},{1,2},{2,3},{3,4},{4,5},{5,6},{6,7},{7,8},{8,9},{9,10},{10,1... | collective-permute-start | bytes 3145736 | tf_op jit(solution)/shard_map/ppermute | solution.py:14
  123.4 4.4 %copy-start.3 = (f32[16,32,32]{2,1,0:T(8,128)S(1)}, f32[16,32,32]{2,1,0:T(8,128)}, u32[]{:S(2)}) copy-start(f32[16,32,32]{2,1,0:T(8,128)} %param.16) | copy-start | bytes 196612
  123.4 4.8 %copy-start.2 = (bf16[16,32,256]{2,1,0:T(8,128)(2,1)S(1)}, bf16[16,32,256]{2,1,0:T(8,128)(2,1)}, u32[]{:S(2)}) copy-start(bf16[16,32,256]{2,1,0:T(8,128)(2,1)} %param.15) | copy-start | bytes 786436
  123.4 6.7 %copy-start.1 = (bf16[4096,128]{1,0:T(8,128)(2,1)S(1)}, bf16[4096,128]{1,0:T(8,128)(2,1)}, u32[]{:S(2)}) copy-start(bf16[4096,128]{1,0:T(8,128)(2,1)} %param.12) | copy-start | bytes 3145732
where the time goes:
time: 155 us; the launch traced here: 154 us
  blocking collectives  89.7 us (58%)
  matrix products  20.3 us (13%)
  starting transfers between devices  17.6 us (11%)
  other arithmetic  15.3 us (10%)
  local copies, waits for them, and re-layouts  11.1 us (7%)
    all_gather x1, blocking collectives, local(): col_coefs = lax.all_gather(top_coef[None], 'col', axis=0, tiled=True)  36.2 us
    psum x1, blocking collectives, local(): top_coef = lax.psum(upward, 'sub')  35 us
    all_gather x1, blocking collectives, local(): sub_coefs = lax.all_gather(cluster_coef[None], 'sub', axis=0, tiled=True)  18.5 us
    ppermute x2, starting transfers between devices, with_halo(): lax.ppermute(lax.slice_in_dim(block, 0, width, axis=dim), axis, backward)  13.7 us
    concatenate x2, other arithmetic, with_halo(): block = jnp.concatenate([low, block, high], axis=dim)  10.8 us
    dot_general x1, matrix products, local(): jnp.einsum('lkij,lkjc->lic', near_blocks, picked, preferred_element_type=...  8.06 us
    gather x1, local copies, waits for them, and re-layouts, local(): picked = window_vec[near_index - window_start]  4.91 us
    dot_general x1, matrix products, local(): jnp.einsum('lkrs,lksc->lrc', leaf_coupling, far_coefs, precision=HIGHEST)  4.43 us
  transfers between devices with their start and end apart: 4, of which 0 were waited for; matrix products, arithmetic and copies ran while one was open for 14% of the time, Pallas kernels for 0%

commit v1 on v0

--- a/solution.py
+++ b/solution.py
@@ -43,7 +43,12 @@
     leaf_coefs = jnp.einsum("lrp,lpc->lrc", leaf_basis, own_vec, preferred_element_type=jnp.float32)
     window_coefs = with_halo(leaf_coefs, ((("col", "sub"), 0),), leaves_here)
     cluster_coef = jnp.einsum("lrs,lrc->sc", leaf_transfer, leaf_coefs, precision=HIGHEST)
-    sub_coefs = lax.all_gather(cluster_coef[None], "sub", axis=0, tiled=True)
+    ring = [cluster_coef[None]]
+    for hop in range(7):
+        ring.append(lax.ppermute(ring[-1], "sub", [(dev, (dev + 1) % 8) for dev in range(8)]))
+    sub_coefs = jnp.roll(
+        jnp.concatenate(ring[::-1], axis=0), (lax.axis_index("sub") + 1) * ring[0].shape[0], axis=0
+    )
     cluster_field = jnp.einsum(
         "krs,ksc->rc", cluster_coupling[0], sub_coefs[cluster_partner[0]], precision=HIGHEST
     )

time: 155 us -> 152 us (0.981)
  the two profiles are of different devices: /device:TPU:1 before, /device:TPU:16 now
where the time goes in v1:
time: 152 us; the launch traced here: 151 us
  blocking collectives  64.4 us (42%)
  waiting for transfers between devices  21.4 us (14%)
  matrix products  20.3 us (13%)
  starting transfers between devices  17.8 us (12%)
  other arithmetic  15.7 us (10%)
  local copies, waits for them, and re-layouts  11.2 us (7%)
    psum x1, blocking collectives, local(): top_coef = lax.psum(upward, 'sub')  40 us
    all_gather x1, blocking collectives, local(): col_coefs = lax.all_gather(top_coef[None], 'col', axis=0, tiled=True)  24.4 us
    ppermute x7, waiting for transfers between devices, local(): lax.ppermute(ring[-1], 'sub', [(dev, (dev + 1) % 8) for dev in range(8)])  21.4 us
    ppermute x2, starting transfers between devices, with_halo(): lax.ppermute(lax.slice_in_dim(block, 0, width, axis=dim), axis, backward)  12.8 us
    concatenate x2, other arithmetic, with_halo(): block = jnp.concatenate([low, block, high], axis=dim)  10.6 us
    dot_general x1, matrix products, local(): jnp.einsum('lkij,lkjc->lic', near_blocks, picked, preferred_element_type=...  8.06 us
    gather x1, local copies, waits for them, and re-layouts, local(): picked = window_vec[near_index - window_start]  4.92 us
    dot_general x1, matrix products, local(): jnp.einsum('lkrs,lksc->lrc', leaf_coupling, far_coefs, precision=HIGHEST)  4.43 us
  transfers between devices with their start and end apart: 11, of which 5 were waited for; matrix products, arithmetic and copies ran while one was open for 14% of the time, Pallas kernels for 0%

profile of v1, /device:TPU:16, one launch (start us, length us, event | category | flops | bytes accessed | tf_op | source)
XLA Modules:
  0.0 151.3 jit_solution(1050901539906467567)
XLA Ops:
  0.0 1.7 %fusion.12 = f32[16,32,128]{2,1,0:T(8,128)S(1)} fusion(bf16[16,32,256]{2,1,0:T(8,128)(2,1)} %param.15, bf16[16,256,128]{2,1,0:T(8,128)(2,1)} %bitcast.82), kind=kOutput, calls=%fused_computation.50 | convolution fusion | flops 33554432 | bytes 1572864 | tf_op jit(solution)/shard_map/lrp,lpc->lrc/dot_general | solution.py:43
  1.7 7.1 %collective-permute-start.3 = (f32[16,32,128]{2,1,0:T(8,128)S(1)}, f32[16,32,128]{2,1,0:T(8,128)S(1)}, u32[]{:S(2)}, u32[]{:S(2)}) collective-permute-start(f32[16,32,128]{2,1,0:T(8,128)S(1)} %fusion.12), channel_id=1, source_target_pairs={{1,0},{2,1},{3,2},{4,3},{5,4},{6,5},{7,6},{8,7},{9,8},{10,9},{11,1... | collective-permute-start | bytes 786440 | tf_op jit(solution)/shard_map/ppermute | solution.py:17
  8.8 1.9 %collective-permute-start.2 = (f32[16,32,128]{2,1,0:T(8,128)S(1)}, f32[16,32,128]{2,1,0:T(8,128)}, u32[]{:S(2)}, u32[]{:S(2)}) collective-permute-start(f32[16,32,128]{2,1,0:T(8,128)S(1)} %fusion.12), channel_id=1, source_target_pairs={{0,1},{1,2},{2,3},{3,4},{4,5},{5,6},{6,7},{7,8},{8,9},{9,10},{10,1... | collective-permute-start | bytes 786440 | tf_op jit(solution)/shard_map/ppermute | solution.py:14
  10.8 5.8 %collective-permute-start.1 = (bf16[4096,128]{1,0:T(8,128)(2,1)}, bf16[4096,128]{1,0:T(8,128)(2,1)}, u32[]{:S(2)}, u32[]{:S(2)}) collective-permute-start(bf16[4096,128]{1,0:T(8,128)(2,1)} %param.12), channel_id=1, source_target_pairs={{1,0},{2,1},{3,2},{4,3},{5,4},{6,5},{7,6},{8,7},{9,8},{10,9},{11,1... | collective-permute-start | bytes 3145736 | tf_op jit(solution)/shard_map/ppermute | solution.py:17
  16.5 1.9 %collective-permute-start = (bf16[4096,128]{1,0:T(8,128)(2,1)}, bf16[4096,128]{1,0:T(8,128)(2,1)}, u32[]{:S(2)}, u32[]{:S(2)}) collective-permute-start(bf16[4096,128]{1,0:T(8,128)(2,1)} %param.12), channel_id=1, source_target_pairs={{0,1},{1,2},{2,3},{3,4},{4,5},{5,6},{6,7},{7,8},{8,9},{9,10},{10,1... | collective-permute-start | bytes 3145736 | tf_op jit(solution)/shard_map/ppermute | solution.py:14
  18.5 1.5 fusion.13
  20.1 1.3 fusion.10
  22.0 1.3 compare_select_fusion.1
  23.2 1.3 compare_select_fusion
  25.4 40.0 %psum.7 = f32[1,32,128]{2,1,0:T(8,128)S(1)} all-reduce(f32[1,32,128]{2,1,0:T(8,128)S(1)} %convolution_bitcast_fusion.3), channel_id=1, replica_groups=mesh['col'=32,'sub'=8] {'sub'}, use_global_device_ids=true, to_apply=%region_0.1 | all-reduce | flops 4096 | bytes 32768 | tf_op jit(solution)/shard_map/psum | solution.py:56
  65.5 1.0 collective-permute-start.5
  66.5 24.4 %all_gather.3 = f32[32,32,128]{2,1,0:T(8,128)S(1)} all-gather(f32[1,32,128]{2,1,0:T(8,128)S(1)} %psum.7), channel_id=1, replica_groups=mesh['col'=32,'sub'=8] {'col'}, dimensions={0}, use_global_device_ids=true | all-gather | bytes 540672 | tf_op jit(solution)/shard_map/all_gather | solution.py:57
  91.5 4.4 %collective-permute-done.6 = f32[1,32,128]{2,1,0:T(8,128)S(1)} collective-permute-done((f32[1,32,128]{2,1,0:T(8,128)S(1)}, f32[1,32,128]{2,1,0:T(8,128)S(1)}, u32[]{:S(2)}, u32[]{:S(2)}) %collective-permute-start.6) | collective-permute-done | bytes 16416 | tf_op jit(solution)/shard_map/ppermute | solution.py:48
  96.2 4.6 %collective-permute-done.7 = f32[1,32,128]{2,1,0:T(8,128)S(1)} collective-permute-done((f32[1,32,128]{2,1,0:T(8,128)S(1)}, f32[1,32,128]{2,1,0:T(8,128)S(1)}, u32[]{:S(2)}, u32[]{:S(2)}) %collective-permute-start.7) | collective-permute-done | bytes 16416 | tf_op jit(solution)/shard_map/ppermute | solution.py:48
  102.4 3.4 %collective-permute-done.8 = f32[1,32,128]{2,1,0:T(8,128)S(1)} collective-permute-done((f32[1,32,128]{2,1,0:T(8,128)S(1)}, f32[1,32,128]{2,1,0:T(8,128)S(1)}, u32[]{:S(2)}, u32[]{:S(2)}) %collective-permute-start.8) | collective-permute-done | bytes 16416 | tf_op jit(solution)/shard_map/ppermute | solution.py:48
  106.6 4.1 %collective-permute-done.9 = f32[1,32,128]{2,1,0:T(8,128)S(1)} collective-permute-done((f32[1,32,128]{2,1,0:T(8,128)S(1)}, f32[1,32,128]{2,1,0:T(8,128)S(1)}, u32[]{:S(2)}, u32[]{:S(2)}) %collective-permute-start.9) | collective-permute-done | bytes 16416 | tf_op jit(solution)/shard_map/ppermute | solution.py:48
  110.7 4.9 %collective-permute-done.10 = f32[1,32,128]{2,1,0:T(8,128)S(1)} collective-permute-done((f32[1,32,128]{2,1,0:T(8,128)S(1)}, f32[1,32,128]{2,1,0:T(8,128)S(1)}, u32[]{:S(2)}, u32[]{:S(2)}) %collective-permute-start.10) | collective-permute-done | bytes 16416 | tf_op jit(solution)/shard_map/ppermute | solution.py:48
  118.6 2.1 %gather_fusion.1 = f32[128,32,128]{2,1,0:T(8,128)} fusion(f32[48,32,128]{2,1,0:T(8,128)S(1)} %pad_maximum_fusion.1, s32[1024]{0:T(1024)S(1)} %pad_clamp_fusion.2), kind=kCustom, calls=%fused_computation.1 | custom fusion | bytes 4194816 | tf_op jit(solution)/shard_map/gather | solution.py:62
  120.7 4.4 %convolution_bitcast_fusion.1 = f32[16,32,128]{2,1,0:T(8,128)S(1)} fusion(f32[16,8,32,128]{3,2,1,0:T(8,128)} %bitcast.81, f32[16,8,32,32]{3,2,1,0:T(8,128)S(1)} %copy-done), kind=kOutput, calls=%fused_computation.10 | convolution fusion | flops 201326592 | bytes 2883584 | tf_op jit(solution)/shard_map/lkrs,lksc->lrc/dot_general | solution.py:63
  125.5 1.9 %fusion.14 = f32[16,128,256]{2,1,0:T(8,128)} fusion(bf16[16,32,128]{2,1,0:T(8,128)(2,1)S(1)} %fusion.3, bf16[16,32,256]{2,1,0:T(8,128)(2,1)S(1)} %copy-done.2), kind=kOutput, calls=%fused_computation.52 | convolution fusion | flops 33554432 | bytes 2490368 | tf_op jit(solution)/shard_map/lrp,lrc->lpc/dot_general | solution.py:72
  127.4 9.6 %pad_maximum_fusion = bf16[12288,128]{1,0:T(8,128)(2,1)} fusion(bf16[4096,128]{1,0:T(8,128)(2,1)} %collective-permute-done.1, bf16[4096,128]{1,0:T(8,128)(2,1)S(1)} %copy-done.1, bf16[4096,128]{1,0:T(8,128)(2,1)} %collective-permute-done), kind=kLoop, calls=%fused_computation.4 | loop fusion | flops 9437184 | bytes 6291456 | tf_op jit(solution)/shard_map/concatenate | solution.py:18
  137.0 4.9 %gather_fusion = bf16[64,256,128]{2,1,0:T(8,128)(2,1)} fusion(bf16[48,256,128]{2,1,0:T(8,128)(2,1)} %bitcast.79, s32[1024]{0:T(1024)S(1)} %pad_clamp_fusion.3), kind=kCustom, calls=%fused_computation | custom fusion | bytes 8388864 | tf_op jit(solution)/shard_map/gather | solution.py:68
  141.9 8.1 %fusion.1 = bf16[16,256,128]{1,2,0:T(8,128)(2,1)S(1)} fusion(f32[16,128,256]{2,1,0:T(8,128)} %fusion.14, bf16[16,4,256,128]{3,2,1,0:T(8,128)(2,1)} %bitcast.80, bf16[16,4,256,256]{3,2,1,0:T(8,128)(2,1)} %param.13), kind=kOutput, calls=%fused_computation.7 | convolution fusion | flops 1074790400 | bytes 15728640 | tf_op jit(solution)/shard_map/lkij,lkjc->lic/dot_general | solution.py:69
  150.0 1.3 copy.26
  (58 shorter events, 8.1 us)
Async XLA Ops:
  0.0 120.7 %copy-start = (f32[16,8,32,32]{3,2,1,0:T(8,128)S(1)}, f32[16,8,32,32]{3,2,1,0:T(8,128)}, u32[]{:S(2)}) copy-start(f32[16,8,32,32]{3,2,1,0:T(8,128)} %param.17) | copy-start | bytes 1572868
  0.0 95.9 %copy-start.4 = (f32[1,8,32,32]{3,2,1,0:T(8,128)S(1)}, f32[1,8,32,32]{3,2,1,0:T(8,128)}, u32[]{:S(2)}) copy-start(f32[1,8,32,32]{3,2,1,0:T(8,128)} %param.22) | copy-start | bytes 98308
  0.0 116.4 %copy-start.5 = (f32[1,4,32,32]{3,2,1,0:T(8,128)S(1)}, f32[1,4,32,32]{3,2,1,0:T(8,128)}, u32[]{:S(2)}) copy-start(f32[1,4,32,32]{3,2,1,0:T(8,128)} %param.20) | copy-start | bytes 49156
  1.7 115.8 %collective-permute-start.3 = (f32[16,32,128]{2,1,0:T(8,128)S(1)}, f32[16,32,128]{2,1,0:T(8,128)S(1)}, u32[]{:S(2)}, u32[]{:S(2)}) collective-permute-start(f32[16,32,128]{2,1,0:T(8,128)S(1)} %fusion.12), channel_id=1, source_target_pairs={{1,0},{2,1},{3,2},{4,3},{5,4},{6,5},{7,6},{8,7},{9,8},{10,9},{11,1... | collective-permute-start | bytes 786440 | tf_op jit(solution)/shard_map/ppermute | solution.py:17
  8.8 108.7 %collective-permute-start.2 = (f32[16,32,128]{2,1,0:T(8,128)S(1)}, f32[16,32,128]{2,1,0:T(8,128)}, u32[]{:S(2)}, u32[]{:S(2)}) collective-permute-start(f32[16,32,128]{2,1,0:T(8,128)S(1)} %fusion.12), channel_id=1, source_target_pairs={{0,1},{1,2},{2,3},{3,4},{4,5},{5,6},{6,7},{7,8},{8,9},{9,10},{10,1... | collective-permute-start | bytes 786440 | tf_op jit(solution)/shard_map/ppermute | solution.py:14
  10.8 116.7 %collective-permute-start.1 = (bf16[4096,128]{1,0:T(8,128)(2,1)}, bf16[4096,128]{1,0:T(8,128)(2,1)}, u32[]{:S(2)}, u32[]{:S(2)}) collective-permute-start(bf16[4096,128]{1,0:T(8,128)(2,1)} %param.12), channel_id=1, source_target_pairs={{1,0},{2,1},{3,2},{4,3},{5,4},{6,5},{7,6},{8,7},{9,8},{10,9},{11,1... | collective-permute-start | bytes 3145736 | tf_op jit(solution)/shard_map/ppermute | solution.py:17
  16.5 110.9 %collective-permute-start = (bf16[4096,128]{1,0:T(8,128)(2,1)}, bf16[4096,128]{1,0:T(8,128)(2,1)}, u32[]{:S(2)}, u32[]{:S(2)}) collective-permute-start(bf16[4096,128]{1,0:T(8,128)(2,1)} %param.12), channel_id=1, source_target_pairs={{0,1},{1,2},{2,3},{3,4},{4,5},{5,6},{6,7},{7,8},{8,9},{9,10},{10,1... | collective-permute-start | bytes 3145736 | tf_op jit(solution)/shard_map/ppermute | solution.py:14
  20.0 45.5 %collective-permute-start.4 = (f32[1,32,128]{2,1,0:T(8,128)S(1)}, f32[1,32,128]{2,1,0:T(8,128)S(1)}, u32[]{:S(2)}, u32[]{:S(2)}) collective-permute-start(f32[1,32,128]{2,1,0:T(8,128)S(1)} %bitcast.83), channel_id=1, source_target_pairs={{0,1},{1,2},{2,3},{3,4},{4,5},{5,6},{6,7},{7,0},{8,9},{9,10},{10,1... | collective-permute-start | bytes 49160 | tf_op jit(solution)/shard_map/ppermute | solution.py:48
  65.5 25.4 %collective-permute-start.5 = (f32[1,32,128]{2,1,0:T(8,128)S(1)}, f32[1,32,128]{2,1,0:T(8,128)S(1)}, u32[]{:S(2)}, u32[]{:S(2)}) collective-permute-start(f32[1,32,128]{2,1,0:T(8,128)S(1)} %collective-permute-done.4), channel_id=1, source_target_pairs={{0,1},{1,2},{2,3},{3,4},{4,5},{5,6},{6,7},{7,0},{8,9},{9,10},{10,1... | collective-permute-start | bytes 49160 | tf_op jit(solution)/shard_map/ppermute | solution.py:48
  90.9 5.0 %collective-permute-start.6 = (f32[1,32,128]{2,1,0:T(8,128)S(1)}, f32[1,32,128]{2,1,0:T(8,128)S(1)}, u32[]{:S(2)}, u32[]{:S(2)}) collective-permute-start(f32[1,32,128]{2,1,0:T(8,128)S(1)} %collective-permute-done.5), channel_id=1, source_target_pairs={{0,1},{1,2},{2,3},{3,4},{4,5},{5,6},{6,7},{7,0},{8,9},{9,10},{10,1... | collective-permute-start | bytes 49160 | tf_op jit(solution)/shard_map/ppermute | solution.py:48
  95.9 4.9 %collective-permute-start.7 = (f32[1,32,128]{2,1,0:T(8,128)S(1)}, f32[1,32,128]{2,1,0:T(8,128)S(1)}, u32[]{:S(2)}, u32[]{:S(2)}) collective-permute-start(f32[1,32,128]{2,1,0:T(8,128)S(1)} %collective-permute-done.6), channel_id=1, source_target_pairs={{0,1},{1,2},{2,3},{3,4},{4,5},{5,6},{6,7},{7,0},{8,9},{9,10},{10,1... | collective-permute-start | bytes 49160 | tf_op jit(solution)/shard_map/ppermute | solution.py:48
  100.8 4.9 %collective-permute-start.8 = (f32[1,32,128]{2,1,0:T(8,128)S(1)}, f32[1,32,128]{2,1,0:T(8,128)S(1)}, u32[]{:S(2)}, u32[]{:S(2)}) collective-permute-start(f32[1,32,128]{2,1,0:T(8,128)S(1)} %collective-permute-done.7), channel_id=1, source_target_pairs={{0,1},{1,2},{2,3},{3,4},{4,5},{5,6},{6,7},{7,0},{8,9},{9,10},{10,1... | collective-permute-start | bytes 49160 | tf_op jit(solution)/shard_map/ppermute | solution.py:48
  105.8 4.9 %collective-permute-start.9 = (f32[1,32,128]{2,1,0:T(8,128)S(1)}, f32[1,32,128]{2,1,0:T(8,128)S(1)}, u32[]{:S(2)}, u32[]{:S(2)}) collective-permute-start(f32[1,32,128]{2,1,0:T(8,128)S(1)} %collective-permute-done.8), channel_id=1, source_target_pairs={{0,1},{1,2},{2,3},{3,4},{4,5},{5,6},{6,7},{7,0},{8,9},{9,10},{10,1... | collective-permute-start | bytes 49160 | tf_op jit(solution)/shard_map/ppermute | solution.py:48
  110.7 5.0 %collective-permute-start.10 = (f32[1,32,128]{2,1,0:T(8,128)S(1)}, f32[1,32,128]{2,1,0:T(8,128)S(1)}, u32[]{:S(2)}, u32[]{:S(2)}) collective-permute-start(f32[1,32,128]{2,1,0:T(8,128)S(1)} %collective-permute-done.9), channel_id=1, source_target_pairs={{0,1},{1,2},{2,3},{3,4},{4,5},{5,6},{6,7},{7,0},{8,9},{9,10},{10,1... | collective-permute-start | bytes 49160 | tf_op jit(solution)/shard_map/ppermute | solution.py:48
  120.7 4.4 %copy-start.3 = (f32[16,32,32]{2,1,0:T(8,128)S(1)}, f32[16,32,32]{2,1,0:T(8,128)}, u32[]{:S(2)}) copy-start(f32[16,32,32]{2,1,0:T(8,128)} %param.16) | copy-start | bytes 196612
  120.7 4.8 %copy-start.2 = (bf16[16,32,256]{2,1,0:T(8,128)(2,1)S(1)}, bf16[16,32,256]{2,1,0:T(8,128)(2,1)}, u32[]{:S(2)}) copy-start(bf16[16,32,256]{2,1,0:T(8,128)(2,1)} %param.15) | copy-start | bytes 786436
  120.7 6.7 %copy-start.1 = (bf16[4096,128]{1,0:T(8,128)(2,1)S(1)}, bf16[4096,128]{1,0:T(8,128)(2,1)}, u32[]{:S(2)}) copy-start(bf16[4096,128]{1,0:T(8,128)(2,1)} %param.12) | copy-start | bytes 3145732
